TPU v7x, 512 devices: a whole 4x8x8 slice. The times are simulated.
512 devices in a mesh: dp: 8 (over y_lo, core), ctx: 64 (over x, y_hi, z).
Axes of the slice: x: 4, y: 8 (y_hi: 2, y_lo: 4; y = y_hi * 4 + y_lo), z: 8, core: 2. Of those that a mesh axis runs over, the one named last changes fastest.
Arguments:
- tokens: bfloat16 [8, 32768, 1024], P('dp', 'ctx'), may hold values from -6 to 6
- w_query: bfloat16 [1024, 1024], P('dp')
- w_key: bfloat16 [1024, 1024], P('dp')
- w_value: bfloat16 [1024, 1024], P('dp'), may hold values from -0.1875 to 0.1875
- w_output: bfloat16 [1024, 1024], P('dp'), may hold values from -0.1875 to 0.1875
- nbr_index: int32 [8, 256, 8], P('dp', 'ctx'), may hold values from 0 to 255, as said below
- nbr_count: int32 [8, 256], P('dp', 'ctx'), may hold values from 1 to 8, as said below
Outputs:
- update: bfloat16 [8, 32768, 1024], P('dp', 'ctx')
Inputs may be any that keep to these rules, and one draw needn't show every extreme that they name: `nbr_index`: in each row the first nbr_count slots name distinct blocks, slot 0 names the query block itself, and every slot names a block at most 8 blocks away from it; unused slots name blocks of that same range. In every draw some block is exactly 8 away from a query block that uses it. `nbr_count`: in every draw some query block uses all 8 slots.
All inputs are finite; a program needn't handle non-finite values.
Results may differ from a plain program's by a relative error of at most 0.0089.
Values may be sent and summed in bfloat16 or wider, within the bound.
No kernel may reach another device: no remote copies, remote signals or barrier semaphores. Data moves between devices by JAX's collectives and lax.ppermute only.
A program may use at most 128 MiB of HBM per device.

v0:
```python
import jax
import jax.numpy as jnp
from jax import lax
from jax.sharding import PartitionSpec as P

HEADS = 8
HD = 128
BLK = 128
MAXN = 8
REACH = 2


def from_behind(value, axis, steps):
    count = lax.axis_size(axis)
    leading, last = (max(0, -steps), min(count, count - steps))
    return lax.ppermute(value, axis, [(source, source + steps) for source in range(leading, last)])


def attend_block(query_blk, key_sel, value_sel, used):
    query_heads = query_blk.reshape(BLK, HEADS, HD)
    key_heads = key_sel.reshape(MAXN * BLK, HEADS, HD)
    value_heads = value_sel.reshape(MAXN * BLK, HEADS, HD)
    scores = jnp.einsum(
        "qhd,khd->hqk", query_heads, key_heads, preferred_element_type=jnp.float32
    ) * HD ** (-0.5)
    slot_used = jnp.arange(MAXN * BLK) // BLK < used
    scores = jnp.where(slot_used[None, None, :], scores, -1e30)
    peak = jnp.max(scores, axis=-1, keepdims=True)
    expo = jnp.exp(scores - peak) * slot_used[None, None, :].astype(jnp.float32)
    weights = (expo / jnp.sum(expo, axis=-1, keepdims=True)).astype(jnp.bfloat16)
    attended = jnp.einsum("hqk,khd->qhd", weights, value_heads, preferred_element_type=jnp.float32)
    return attended.reshape(BLK, HEADS * HD).astype(jnp.bfloat16)


def move_far(payload, offset):
    return from_behind((payload[0], payload[1]), "ctx", offset)


def collect_window(payload):
    lower = []
    upper = []
    for offset in list(range(REACH, 0, -1)) + list(range(-1, -REACH - 1, -1)):
        moved = move_far(payload, offset)
        if offset > 0:
            lower.append(moved)
        else:
            upper.append(moved)
    return (lower, upper)


def project_pair(rows_in, full_key, full_value):
    keys = jnp.dot(rows_in, full_key, preferred_element_type=jnp.float32).astype(jnp.bfloat16)
    values = jnp.dot(rows_in, full_value, preferred_element_type=jnp.float32).astype(jnp.bfloat16)
    return (keys, values)


def gather_window(keys, values):
    lower, upper = collect_window((keys, values))
    pieces = lower + [(keys, values)] + upper
    key_window = jnp.concatenate([item[0] for item in pieces], axis=0)
    value_window = jnp.concatenate([item[1] for item in pieces], axis=0)
    return (key_window, value_window)


def body(tokens, w_query, w_key, w_value, w_output, nbr_index, nbr_count):
    local_tok = tokens[0]
    blocks = local_tok.shape[0] // BLK
    rank = lax.axis_index("ctx")
    values_f = local_tok.astype(jnp.float32)
    normed = (
        values_f * lax.rsqrt(jnp.mean(values_f * values_f, axis=-1, keepdims=True) + 1e-05)
    ).astype(jnp.bfloat16)
    full_query, full_key, full_value, full_output = (
        lax.all_gather(w_query, "dp", axis=0, tiled=True),
        lax.all_gather(w_key, "dp", axis=0, tiled=True),
        lax.all_gather(w_value, "dp", axis=0, tiled=True),
        lax.all_gather(w_output, "dp", axis=0, tiled=True),
    )
    keys, values = project_pair(normed, full_key, full_value)
    key_window, value_window = gather_window(keys, values)
    queries = jnp.dot(normed, full_query, preferred_element_type=jnp.float32).astype(jnp.bfloat16)
    width = HEADS * HD
    key_blocks = key_window.reshape(-1, BLK, width)
    value_blocks = value_window.reshape(-1, BLK, width)
    first_block = rank * blocks - REACH * blocks
    local_index = nbr_index[0] - first_block
    query_blocks = queries.reshape(blocks, BLK, width)

    def per_block(items):
        query_blk, index_row, used = items
        key_sel = jnp.take(key_blocks, index_row, axis=0)
        value_sel = jnp.take(value_blocks, index_row, axis=0)
        return attend_block(query_blk, key_sel, value_sel, used)

    attended = lax.map(per_block, (query_blocks, local_index, nbr_count[0])).reshape(
        blocks * BLK, width
    )
    update = jnp.dot(attended, full_output, preferred_element_type=jnp.float32).astype(jnp.bfloat16)
    return update[None]


def solution(mesh):
    placed = (
        P("dp", "ctx", None),
        P("dp", None),
        P("dp", None),
        P("dp", None),
        P("dp", None),
        P("dp", "ctx", None),
        P("dp", "ctx"),
    )
    return jax.shard_map(
        body, mesh=mesh, in_specs=placed, out_specs=P("dp", "ctx", None), check_vma=False
    )
```

profile of v0, /device:TPU:59, one launch (start us, length us, event | category | flops | bytes accessed | tf_op | source)
XLA Modules:
  0.0 534.2 jit_solution(2425077717888437057)
XLA Ops:
  8.8 1.5 fusion.20
  10.3 45.3 %all-gather.9.cloned.1.call-done = bf16[1024,1024]{1,0:T(8,128)(2,1)} async-done(((bf16[128,1024]{1,0:T(8,128)(2,1)}), bf16[1024,1024]{1,0:T(8,128)(2,1)}) %all-gather.9.cloned.1.call-update) | async-done | bytes 2097168 | tf_op jit(solution)/shard_map/all_gather | solution.py:75
  55.6 3.2 convolution_convert_fusion.1
  58.8 4.3 collective-permute-start.4
  63.2 3.3 collective-permute-start.5
  66.5 33.6 %all-gather.5.cloned.1.call-done = bf16[1024,1024]{1,0:T(8,128)(2,1)} async-done(((bf16[128,1024]{1,0:T(8,128)(2,1)}), bf16[1024,1024]{1,0:T(8,128)(2,1)}) %all-gather.5.cloned.1.call-update) | async-done | bytes 2097168 | tf_op jit(solution)/shard_map/all_gather | solution.py:76
  100.0 2.9 convolution_convert_fusion.3
  102.9 3.4 collective-permute-start
  106.4 3.3 collective-permute-start.1
  109.7 76.0 %collective-permute-start.6 = (bf16[512,1024]{1,0:T(8,128)(2,1)S(1)}, bf16[512,1024]{1,0:T(8,128)(2,1)}, u32[]{:S(2)}, u32[]{:S(2)}) collective-permute-start(bf16[512,1024]{1,0:T(8,128)(2,1)S(1)} %convolution_convert_fusion.1), channel_id=1, source_target_pairs={{1,0},{2,1},{3,2},{4,3},{5,4},{6,5},{7,6},{8,7},{9,8},{10,9},{11,1... | collective-permute-start | bytes 3145736 | tf_op jit(solution)/shard_map/ppermute | solution.py:16
  185.7 4.3 collective-permute-start.7
  190.0 59.2 %all-gather.7.cloned.1.call-done = bf16[1024,1024]{1,0:T(8,128)(2,1)} async-done(((bf16[128,1024]{1,0:T(8,128)(2,1)}), bf16[1024,1024]{1,0:T(8,128)(2,1)}) %all-gather.7.cloned.1.call-update) | async-done | bytes 2097168 | tf_op jit(solution)/shard_map/all_gather | solution.py:74
  249.1 3.9 convolution_convert_fusion.2
  253.0 62.1 %collective-permute-start.2 = (bf16[512,1024]{1,0:T(8,128)(2,1)S(1)}, bf16[512,1024]{1,0:T(8,128)(2,1)S(1)}, u32[]{:S(2)}, u32[]{:S(2)}) collective-permute-start(bf16[512,1024]{1,0:T(8,128)(2,1)S(1)} %convolution_convert_fusion.3), channel_id=1, source_target_pairs={{1,0},{2,1},{3,2},{4,3},{5,4},{6,5},{7,6},{8,7},{9,8},{10,9},{11,1... | collective-permute-start | bytes 3145736 | tf_op jit(solution)/shard_map/ppermute | solution.py:16
  315.1 1.3 constant_dynamic-update-slice_fusion.10
  316.4 1.9 collective-permute-start.3
  318.3 1.3 constant_dynamic-update-slice_fusion.9
  319.7 1.3 constant_dynamic-update-slice_fusion.5
  321.0 1.3 constant_dynamic-update-slice_fusion.4
  322.4 1.3 constant_dynamic-update-slice_fusion.7
  323.7 1.3 constant_dynamic-update-slice_fusion.6
  325.0 97.5 %collective-permute-done.2 = bf16[512,1024]{1,0:T(8,128)(2,1)S(1)} collective-permute-done((bf16[512,1024]{1,0:T(8,128)(2,1)S(1)}, bf16[512,1024]{1,0:T(8,128)(2,1)S(1)}, u32[]{:S(2)}, u32[]{:S(2)}) %collective-permute-start.2) | collective-permute-done | bytes 1048608 | tf_op jit(solution)/shard_map/ppermute | solution.py:16
  422.6 21.2 %collective-permute-done.3 = bf16[512,1024]{1,0:T(8,128)(2,1)S(1)} collective-permute-done((bf16[512,1024]{1,0:T(8,128)(2,1)S(1)}, bf16[512,1024]{1,0:T(8,128)(2,1)S(1)}, u32[]{:S(2)}, u32[]{:S(2)}) %collective-permute-start.3) | collective-permute-done | bytes 1048608 | tf_op jit(solution)/shard_map/ppermute | solution.py:16
  443.9 2.3 copy-done.2
  446.2 77.2 %while.12 = (s32[]{:T(128)}, bf16[4,128,1024]{2,1,0:T(8,128)(2,1)}, s32[4,8]{1,0:T(4,128)S(1)}, bf16[20,128,1024]{2,1,0:T(8,128)(2,1)}, s32[4]{0:T(128)S(1)}, /*...) while((s32[]{:T(128)}, bf16[4,128,1024]{2,1,0:T(8,128)(2,1)}, ...), condition=%wide.region_4.6_spmd, body=%wide.region_1.5_spmd.sunk | while | flops 548548672 | bytes 57170744 | solution.py:95
  446.3 3.2 gather_fusion
  449.4 4.5 gather_fusion.1
  453.9 3.4 broadcast_select_fusion.3
  457.9 1.0 constant_dynamic-slice_fusion.3
  461.1 1.7 fusion.45
  463.4 1.3 fusion.46
  465.6 3.2 gather_fusion
  468.7 4.5 gather_fusion.1
  473.2 3.4 broadcast_select_fusion.3
  480.4 1.7 fusion.45
  482.7 1.3 fusion.46
  484.9 3.2 gather_fusion
  488.1 4.5 gather_fusion.1
  492.6 3.4 broadcast_select_fusion.3
  496.5 1.0 constant_dynamic-slice_fusion.3
  499.7 1.7 fusion.45
  502.0 1.3 fusion.46
  504.2 3.2 gather_fusion
  507.4 4.5 gather_fusion.1
  511.9 3.4 broadcast_select_fusion.3
  519.0 1.7 fusion.45
  521.3 1.3 fusion.46
  523.5 4.1 fusion.22
  (81 shorter events, 21.6 us)
Async XLA Ops:
  6.5 49.1 %all-gather.9.cloned.1.call-start = ((), (), s32[]{:S(2)}) async-start(), calls=%async_computation.2 | async-start | bytes 2359296 | tf_op jit(solution)/shard_map/all_gather | solution.py:75
  7.3 92.8 %all-gather.5.cloned.1.call-start = ((), (), s32[]{:S(2)}) async-start(), calls=%async_computation | async-start | bytes 2359296 | tf_op jit(solution)/shard_map/all_gather | solution.py:76
  8.0 241.1 %all-gather.7.cloned.1.call-start = ((), (), s32[]{:S(2)}) async-start(), calls=%async_computation.1 | async-start | bytes 2359296 | tf_op jit(solution)/shard_map/all_gather | solution.py:74
  8.7 514.8 %all-gather.11.cloned.1.call-start = ((), (), s32[]{:S(2)}) async-start(), calls=%async_computation.3 | async-start | bytes 2359296 | tf_op jit(solution)/shard_map/all_gather | solution.py:77
  10.3 89.7 %copy-start.3 = (bf16[1,512,1024]{2,1,0:T(8,128)(2,1)S(1)}, bf16[1,512,1024]{2,1,0:T(8,128)(2,1)}, u32[]{:S(2)}) copy-start(bf16[1,512,1024]{2,1,0:T(8,128)(2,1)} %param.11) | copy-start | bytes 3145732
  58.8 50.9 %copy-start.4 = (s32[1,4,8]{2,1,0:T(4,128)S(1)}, s32[1,4,8]{2,1,0:T(4,128)}, u32[]{:S(2)}) copy-start(s32[1,4,8]{2,1,0:T(4,128)} %param.16) | copy-start | bytes 388
  58.8 126.9 %collective-permute-start.4 = (bf16[512,1024]{1,0:T(8,128)(2,1)S(1)}, bf16[512,1024]{1,0:T(8,128)(2,1)}, u32[]{:S(2)}, u32[]{:S(2)}) collective-permute-start(bf16[512,1024]{1,0:T(8,128)(2,1)S(1)} %convolution_convert_fusion.1), channel_id=1, source_target_pairs={{0,2},{1,3},{2,4},{3,5},{4,6},{5,7},{6,8},{7,9},{8,10},{9,11},{10,... | collective-permute-start | bytes 3145736 | tf_op jit(solution)/shard_map/ppermute | solution.py:16
  63.2 189.8 %collective-permute-start.5 = (bf16[512,1024]{1,0:T(8,128)(2,1)S(1)}, bf16[512,1024]{1,0:T(8,128)(2,1)}, u32[]{:S(2)}, u32[]{:S(2)}) collective-permute-start(bf16[512,1024]{1,0:T(8,128)(2,1)S(1)} %convolution_convert_fusion.1), channel_id=1, source_target_pairs={{0,1},{1,2},{2,3},{3,4},{4,5},{5,6},{6,7},{7,8},{8,9},{9,10},{10,1... | collective-permute-start | bytes 3145736 | tf_op jit(solution)/shard_map/ppermute | solution.py:16
  102.9 213.5 %collective-permute-start = (bf16[512,1024]{1,0:T(8,128)(2,1)S(1)}, bf16[512,1024]{1,0:T(8,128)(2,1)}, u32[]{:S(2)}, u32[]{:S(2)}) collective-permute-start(bf16[512,1024]{1,0:T(8,128)(2,1)S(1)} %convolution_convert_fusion.3), channel_id=1, source_target_pairs={{0,2},{1,3},{2,4},{3,5},{4,6},{5,7},{6,8},{7,9},{8,10},{9,11},{10,... | collective-permute-start | bytes 3145736 | tf_op jit(solution)/shard_map/ppermute | solution.py:16
  106.4 214.6 %collective-permute-start.1 = (bf16[512,1024]{1,0:T(8,128)(2,1)S(1)}, bf16[512,1024]{1,0:T(8,128)(2,1)}, u32[]{:S(2)}, u32[]{:S(2)}) collective-permute-start(bf16[512,1024]{1,0:T(8,128)(2,1)S(1)} %convolution_convert_fusion.3), channel_id=1, source_target_pairs={{0,1},{1,2},{2,3},{3,4},{4,5},{5,6},{6,7},{7,8},{8,9},{9,10},{10,1... | collective-permute-start | bytes 3145736 | tf_op jit(solution)/shard_map/ppermute | solution.py:16
  109.7 212.7 %collective-permute-start.6 = (bf16[512,1024]{1,0:T(8,128)(2,1)S(1)}, bf16[512,1024]{1,0:T(8,128)(2,1)}, u32[]{:S(2)}, u32[]{:S(2)}) collective-permute-start(bf16[512,1024]{1,0:T(8,128)(2,1)S(1)} %convolution_convert_fusion.1), channel_id=1, source_target_pairs={{1,0},{2,1},{3,2},{4,3},{5,4},{6,5},{7,6},{8,7},{9,8},{10,9},{11,1... | collective-permute-start | bytes 3145736 | tf_op jit(solution)/shard_map/ppermute | solution.py:16
  185.7 138.0 %collective-permute-start.7 = (bf16[512,1024]{1,0:T(8,128)(2,1)S(1)}, bf16[512,1024]{1,0:T(8,128)(2,1)}, u32[]{:S(2)}, u32[]{:S(2)}) collective-permute-start(bf16[512,1024]{1,0:T(8,128)(2,1)S(1)} %convolution_convert_fusion.1), channel_id=1, source_target_pairs={{2,0},{3,1},{4,2},{5,3},{6,4},{7,5},{8,6},{9,7},{10,8},{11,9},{12,... | collective-permute-start | bytes 3145736 | tf_op jit(solution)/shard_map/ppermute | solution.py:16
  253.0 169.6 %collective-permute-start.2 = (bf16[512,1024]{1,0:T(8,128)(2,1)S(1)}, bf16[512,1024]{1,0:T(8,128)(2,1)S(1)}, u32[]{:S(2)}, u32[]{:S(2)}) collective-permute-start(bf16[512,1024]{1,0:T(8,128)(2,1)S(1)} %convolution_convert_fusion.3), channel_id=1, source_target_pairs={{1,0},{2,1},{3,2},{4,3},{5,4},{6,5},{7,6},{8,7},{9,8},{10,9},{11,1... | collective-permute-start | bytes 3145736 | tf_op jit(solution)/shard_map/ppermute | solution.py:16
  316.4 127.4 %collective-permute-start.3 = (bf16[512,1024]{1,0:T(8,128)(2,1)S(1)}, bf16[512,1024]{1,0:T(8,128)(2,1)S(1)}, u32[]{:S(2)}, u32[]{:S(2)}) collective-permute-start(bf16[512,1024]{1,0:T(8,128)(2,1)S(1)} %convolution_convert_fusion.3), channel_id=1, source_target_pairs={{2,0},{3,1},{4,2},{5,3},{6,4},{7,5},{8,6},{9,7},{10,8},{11,9},{12,... | collective-permute-start | bytes 3145736 | tf_op jit(solution)/shard_map/ppermute | solution.py:16
  325.0 118.9 %copy-start.1 = (bf16[2560,1024]{1,0:T(8,128)(2,1)}, bf16[2560,1024]{1,0:T(8,128)(2,1)S(1)}, u32[]{:S(2)}) copy-start(bf16[2560,1024]{1,0:T(8,128)(2,1)S(1)} %constant_dynamic-update-slice_fusion.6) | copy-start | bytes 15728644
  325.0 121.2 %copy-start.5 = (s32[1,4]{1,0:T(1,128)S(1)}, s32[1,4]{1,0:T(1,128)}, u32[]{:S(2)}) copy-start(s32[1,4]{1,0:T(1,128)} %param.17) | copy-start | bytes 52
  443.9 2.3 copy-start.2
  461.1 1.7 copy-start
  480.4 1.7 copy-start
  499.7 1.7 copy-start
  519.0 1.7 copy-start
Sparse Core Ops, SparseCore 0:
  9.4 46.1 all-gather.8
  57.7 42.3 all-gather.4
  102.1 146.9 all-gather.6
  251.1 170.1 all-gather.10
where the time goes:
time: 535 us; the launch traced here: 534 us
  waiting for transfers between devices  259 us (48%)
  starting transfers between devices  159 us (30%)
  local copies, waits for them, and re-layouts  56.4 us (11%)
  other arithmetic  24.2 us (5%)
  matrix products  22.3 us (4%)
  between operations  13.4 us (3%)
    ppermute x8, starting transfers between devices, from_behind(): lax.ppermute(value, axis, [(source, source + steps) for source in range(l...  159 us
    ppermute x8, waiting for transfers between devices, from_behind(): lax.ppermute(value, axis, [(source, source + steps) for source in range(l...  119 us
    all_gather x1, waiting for transfers between devices, body(): lax.all_gather(w_query, 'dp', axis=0, tiled=True)  59.2 us
    all_gather x1, waiting for transfers between devices, body(): lax.all_gather(w_key, 'dp', axis=0, tiled=True)  45.3 us
    all_gather x1, waiting for transfers between devices, body(): lax.all_gather(w_value, 'dp', axis=0, tiled=True)  33.6 us
    gather x4, local copies, waits for them, and re-layouts, per_block(): key_sel = jnp.take(key_blocks, index_row, axis=0)  18 us
    select_n x4, other arithmetic, per_block(): value_sel = jnp.take(value_blocks, index_row, axis=0)  13.4 us
    gather x4, local copies, waits for them, and re-layouts, per_block(): value_sel = jnp.take(value_blocks, index_row, axis=0)  12.7 us
  transfers between devices with their start and end apart: 12, of which 5 were waited for; matrix products, arithmetic and copies ran while one was open for 18% of the time, Pallas kernels for 0%

commit v1 on v0

--- a/solution.py
+++ b/solution.py
@@ -73,7 +73,9 @@
     full_query, full_key, full_value, full_output = (
         lax.all_gather(w_query, "dp", axis=0, tiled=True),
         lax.all_gather(w_key, "dp", axis=0, tiled=True),
-        lax.all_gather(w_value, "dp", axis=0, tiled=True),
+        jnp.concatenate(
+            lax.all_to_all(jnp.stack([w_value] * lax.axis_size("dp")), "dp", 0, 0), axis=0
+        ),
         lax.all_gather(w_output, "dp", axis=0, tiled=True),
     )
     keys, values = project_pair(normed, full_key, full_value)

time: 535 us -> 552 us (1.032)
  the two profiles are of different devices: /device:TPU:59 before, /device:TPU:44 now
where the time goes in v1:
time: 552 us; the launch traced here: 551 us
  waiting for transfers between devices  330 us (60%)
  starting transfers between devices  102 us (18%)
  local copies, waits for them, and re-layouts  58.9 us (11%)
  other arithmetic  23.1 us (4%)
  matrix products  22.4 us (4%)
  between operations  13.3 us (2%)
    ppermute x8, waiting for transfers between devices, from_behind(): lax.ppermute(value, axis, [(source, source + steps) for source in range(l...  263 us
    ppermute x8, starting transfers between devices, from_behind(): lax.ppermute(value, axis, [(source, source + steps) for source in range(l...  97 us
    all_gather x1, waiting for transfers between devices, body(): lax.all_gather(w_key, 'dp', axis=0, tiled=True)  66.2 us
    gather x4, local copies, waits for them, and re-layouts, per_block(): key_sel = jnp.take(key_blocks, index_row, axis=0)  18 us
    select_n x4, other arithmetic, per_block(): value_sel = jnp.take(value_blocks, index_row, axis=0)  13.5 us
    gather x4, local copies, waits for them, and re-layouts, per_block(): value_sel = jnp.take(value_blocks, index_row, axis=0)  12.7 us
  transfers between devices with their start and end apart: 12, of which 5 were waited for; matrix products, arithmetic and copies ran while one was open for 18% of the time, Pallas kernels for 0%

profile of v1, /device:TPU:44, one launch (start us, length us, event | category | flops | bytes accessed | tf_op | source)
XLA Modules:
  0.0 550.6 jit_solution(10894884629813526581)
XLA Ops:
  7.3 2.5 stack.2
  9.8 5.0 all-to-all-start
  15.9 66.2 %all-gather.6.cloned.1.call-done = bf16[1024,1024]{1,0:T(8,128)(2,1)} async-done(((bf16[128,1024]{1,0:T(8,128)(2,1)}), bf16[1024,1024]{1,0:T(8,128)(2,1)}) %all-gather.6.cloned.1.call-update) | async-done | bytes 2097168 | tf_op jit(solution)/shard_map/all_gather | solution.py:75
  82.0 3.9 convolution_convert_fusion.1
  85.9 5.9 %collective-permute-start.4 = (bf16[512,1024]{1,0:T(8,128)(2,1)}, bf16[512,1024]{1,0:T(8,128)(2,1)}, u32[]{:S(2)}, u32[]{:S(2)}) collective-permute-start(bf16[512,1024]{1,0:T(8,128)(2,1)} %convolution_convert_fusion.1), channel_id=1, source_target_pairs={{0,2},{1,3},{2,4},{3,5},{4,6},{5,7},{6,8},{7,9},{8,10},{9,11},{10,... | collective-permute-start | bytes 3145736 | tf_op jit(solution)/shard_map/ppermute | solution.py:16
  91.9 4.1 collective-permute-start.5
  96.0 2.3 convolution_convert_fusion.3
  98.3 5.8 %collective-permute-start = (bf16[512,1024]{1,0:T(8,128)(2,1)}, bf16[512,1024]{1,0:T(8,128)(2,1)S(1)}, u32[]{:S(2)}, u32[]{:S(2)}) collective-permute-start(bf16[512,1024]{1,0:T(8,128)(2,1)} %convolution_convert_fusion.3), channel_id=1, source_target_pairs={{0,2},{1,3},{2,4},{3,5},{4,6},{5,7},{6,8},{7,9},{8,10},{9,11},{10,... | collective-permute-start | bytes 3145736 | tf_op jit(solution)/shard_map/ppermute | solution.py:16
  104.1 3.0 collective-permute-start.1
  107.2 8.8 %collective-permute-start.6 = (bf16[512,1024]{1,0:T(8,128)(2,1)}, bf16[512,1024]{1,0:T(8,128)(2,1)S(1)}, u32[]{:S(2)}, u32[]{:S(2)}) collective-permute-start(bf16[512,1024]{1,0:T(8,128)(2,1)} %convolution_convert_fusion.1), channel_id=1, source_target_pairs={{1,0},{2,1},{3,2},{4,3},{5,4},{6,5},{7,6},{8,7},{9,8},{10,9},{11,1... | collective-permute-start | bytes 3145736 | tf_op jit(solution)/shard_map/ppermute | solution.py:16
  116.0 100.6 %collective-permute-done.4 = bf16[512,1024]{1,0:T(8,128)(2,1)} collective-permute-done((bf16[512,1024]{1,0:T(8,128)(2,1)}, bf16[512,1024]{1,0:T(8,128)(2,1)}, u32[]{:S(2)}, u32[]{:S(2)}) %collective-permute-start.4) | collective-permute-done | bytes 1048608 | tf_op jit(solution)/shard_map/ppermute | solution.py:16
  216.7 1.9 collective-permute-start.7
  218.6 3.9 convolution_convert_fusion.2
  222.5 63.5 %collective-permute-done.5 = bf16[512,1024]{1,0:T(8,128)(2,1)} collective-permute-done((bf16[512,1024]{1,0:T(8,128)(2,1)}, bf16[512,1024]{1,0:T(8,128)(2,1)}, u32[]{:S(2)}, u32[]{:S(2)}) %collective-permute-start.5) | collective-permute-done | bytes 1048608 | tf_op jit(solution)/shard_map/ppermute | solution.py:16
  286.0 65.5 %collective-permute-start.2 = (bf16[512,1024]{1,0:T(8,128)(2,1)}, bf16[512,1024]{1,0:T(8,128)(2,1)S(1)}, u32[]{:S(2)}, u32[]{:S(2)}) collective-permute-start(bf16[512,1024]{1,0:T(8,128)(2,1)} %convolution_convert_fusion.3), channel_id=1, source_target_pairs={{1,0},{2,1},{3,2},{4,3},{5,4},{6,5},{7,6},{8,7},{9,8},{10,9},{11,1... | collective-permute-start | bytes 3145736 | tf_op jit(solution)/shard_map/ppermute | solution.py:16
  351.5 1.3 constant_dynamic-update-slice_fusion.10
  352.8 1.9 collective-permute-start.3
  354.7 1.3 constant_dynamic-update-slice_fusion.9
  356.0 1.3 constant_dynamic-update-slice_fusion.8
  357.4 1.3 constant_dynamic-update-slice_fusion.4
  358.7 1.3 constant_dynamic-update-slice_fusion.3
  360.1 1.3 constant_dynamic-update-slice_fusion.6
  361.4 78.6 %collective-permute-done.2 = bf16[512,1024]{1,0:T(8,128)(2,1)S(1)} collective-permute-done((bf16[512,1024]{1,0:T(8,128)(2,1)}, bf16[512,1024]{1,0:T(8,128)(2,1)S(1)}, u32[]{:S(2)}, u32[]{:S(2)}) %collective-permute-start.2) | collective-permute-done | bytes 1048608 | tf_op jit(solution)/shard_map/ppermute | solution.py:16
  440.0 20.1 %collective-permute-done.3 = bf16[512,1024]{1,0:T(8,128)(2,1)S(1)} collective-permute-done((bf16[512,1024]{1,0:T(8,128)(2,1)}, bf16[512,1024]{1,0:T(8,128)(2,1)S(1)}, u32[]{:S(2)}, u32[]{:S(2)}) %collective-permute-start.3) | collective-permute-done | bytes 1048608 | tf_op jit(solution)/shard_map/ppermute | solution.py:16
  460.2 2.3 copy-done.2
  462.5 77.4 %while.12 = (s32[]{:T(128)}, bf16[4,128,1024]{2,1,0:T(8,128)(2,1)}, s32[4,8]{1,0:T(4,128)S(1)}, bf16[20,128,1024]{2,1,0:T(8,128)(2,1)}, s32[4]{0:T(128)S(1)}, /*...) while((s32[]{:T(128)}, bf16[4,128,1024]{2,1,0:T(8,128)(2,1)}, ...), condition=%wide.region_4.6_spmd, body=%wide.region_1.5_spmd.sunk | while | flops 548548672 | bytes 57170744 | solution.py:97
  462.5 3.2 gather_fusion
  465.7 4.5 gather_fusion.1
  470.2 3.4 broadcast_select_fusion.3
  474.2 1.0 constant_dynamic-slice_fusion.3
  477.4 1.7 fusion.50
  479.7 1.3 fusion.51
  481.9 3.2 gather_fusion
  485.0 4.5 gather_fusion.1
  489.5 3.4 broadcast_select_fusion.3
  496.7 1.7 fusion.50
  499.0 1.3 fusion.51
  501.2 3.2 gather_fusion
  504.4 4.5 gather_fusion.1
  508.9 3.4 broadcast_select_fusion.3
  516.1 1.7 fusion.50
  518.4 1.3 fusion.51
  520.6 3.2 gather_fusion
  523.8 4.5 gather_fusion.1
  528.3 3.4 broadcast_select_fusion.3
  535.4 1.7 fusion.50
  537.7 1.3 fusion.51
  539.9 4.1 fusion.25
  (81 shorter events, 22.2 us)
Async XLA Ops:
  6.5 75.5 %all-gather.6.cloned.1.call-start = ((), (), s32[]{:S(2)}) async-start(), calls=%async_computation.2 | async-start | bytes 2359296 | tf_op jit(solution)/shard_map/all_gather | solution.py:75
  9.8 5.8 %copy-start.3 = (bf16[1,512,1024]{2,1,0:T(8,128)(2,1)S(1)}, bf16[1,512,1024]{2,1,0:T(8,128)(2,1)}, u32[]{:S(2)}) copy-start(bf16[1,512,1024]{2,1,0:T(8,128)(2,1)} %param.11) | copy-start | bytes 3145732
  9.8 86.2 %all-to-all-start = ((bf16[8,128,1024]{2,1,0:T(8,128)(2,1)}), bf16[8,128,1024]{2,1,0:T(8,128)(2,1)S(1)}, u32[]{:S(2)}, u32[]{:S(2)}) async-start(bf16[8,128,1024]{2,1,0:T(8,128)(2,1)} %stack.2), calls=%async_computation | async-start | bytes 4194304 | tf_op jit(solution)/shard_map/all_to_all | solution.py:77
  14.8 203.8 %all-gather.4.cloned.1.call-start = ((), (), s32[]{:S(2)}) async-start(), calls=%async_computation.1 | async-start | bytes 2359296 | tf_op jit(solution)/shard_map/all_gather | solution.py:74
  15.5 524.4 %all-gather.8.cloned.1.call-start = ((), (), s32[]{:S(2)}) async-start(), calls=%async_computation.3 | async-start | bytes 2359296 | tf_op jit(solution)/shard_map/all_gather | solution.py:79
  85.9 130.7 %collective-permute-start.4 = (bf16[512,1024]{1,0:T(8,128)(2,1)}, bf16[512,1024]{1,0:T(8,128)(2,1)}, u32[]{:S(2)}, u32[]{:S(2)}) collective-permute-start(bf16[512,1024]{1,0:T(8,128)(2,1)} %convolution_convert_fusion.1), channel_id=1, source_target_pairs={{0,2},{1,3},{2,4},{3,5},{4,6},{5,7},{6,8},{7,9},{8,10},{9,11},{10,... | collective-permute-start | bytes 3145736 | tf_op jit(solution)/shard_map/ppermute | solution.py:16
  91.9 194.1 %collective-permute-start.5 = (bf16[512,1024]{1,0:T(8,128)(2,1)}, bf16[512,1024]{1,0:T(8,128)(2,1)}, u32[]{:S(2)}, u32[]{:S(2)}) collective-permute-start(bf16[512,1024]{1,0:T(8,128)(2,1)} %convolution_convert_fusion.1), channel_id=1, source_target_pairs={{0,1},{1,2},{2,3},{3,4},{4,5},{5,6},{6,7},{7,8},{8,9},{9,10},{10,1... | collective-permute-start | bytes 3145736 | tf_op jit(solution)/shard_map/ppermute | solution.py:16
  96.0 11.2 %copy-start.4 = (s32[1,4,8]{2,1,0:T(4,128)S(1)}, s32[1,4,8]{2,1,0:T(4,128)}, u32[]{:S(2)}) copy-start(s32[1,4,8]{2,1,0:T(4,128)} %param.16) | copy-start | bytes 388
  98.3 254.5 %collective-permute-start = (bf16[512,1024]{1,0:T(8,128)(2,1)}, bf16[512,1024]{1,0:T(8,128)(2,1)S(1)}, u32[]{:S(2)}, u32[]{:S(2)}) collective-permute-start(bf16[512,1024]{1,0:T(8,128)(2,1)} %convolution_convert_fusion.3), channel_id=1, source_target_pairs={{0,2},{1,3},{2,4},{3,5},{4,6},{5,7},{6,8},{7,9},{8,10},{9,11},{10,... | collective-permute-start | bytes 3145736 | tf_op jit(solution)/shard_map/ppermute | solution.py:16
  104.1 253.2 %collective-permute-start.1 = (bf16[512,1024]{1,0:T(8,128)(2,1)}, bf16[512,1024]{1,0:T(8,128)(2,1)}, u32[]{:S(2)}, u32[]{:S(2)}) collective-permute-start(bf16[512,1024]{1,0:T(8,128)(2,1)} %convolution_convert_fusion.3), channel_id=1, source_target_pairs={{0,1},{1,2},{2,3},{3,4},{4,5},{5,6},{6,7},{7,8},{8,9},{9,10},{10,1... | collective-permute-start | bytes 3145736 | tf_op jit(solution)/shard_map/ppermute | solution.py:16
  107.2 252.7 %collective-permute-start.6 = (bf16[512,1024]{1,0:T(8,128)(2,1)}, bf16[512,1024]{1,0:T(8,128)(2,1)S(1)}, u32[]{:S(2)}, u32[]{:S(2)}) collective-permute-start(bf16[512,1024]{1,0:T(8,128)(2,1)} %convolution_convert_fusion.1), channel_id=1, source_target_pairs={{1,0},{2,1},{3,2},{4,3},{5,4},{6,5},{7,6},{8,7},{9,8},{10,9},{11,1... | collective-permute-start | bytes 3145736 | tf_op jit(solution)/shard_map/ppermute | solution.py:16
  216.7 143.4 %collective-permute-start.7 = (bf16[512,1024]{1,0:T(8,128)(2,1)}, bf16[512,1024]{1,0:T(8,128)(2,1)}, u32[]{:S(2)}, u32[]{:S(2)}) collective-permute-start(bf16[512,1024]{1,0:T(8,128)(2,1)} %convolution_convert_fusion.1), channel_id=1, source_target_pairs={{2,0},{3,1},{4,2},{5,3},{6,4},{7,5},{8,6},{9,7},{10,8},{11,9},{12,... | collective-permute-start | bytes 3145736 | tf_op jit(solution)/shard_map/ppermute | solution.py:16
  286.0 154.0 %collective-permute-start.2 = (bf16[512,1024]{1,0:T(8,128)(2,1)}, bf16[512,1024]{1,0:T(8,128)(2,1)S(1)}, u32[]{:S(2)}, u32[]{:S(2)}) collective-permute-start(bf16[512,1024]{1,0:T(8,128)(2,1)} %convolution_convert_fusion.3), channel_id=1, source_target_pairs={{1,0},{2,1},{3,2},{4,3},{5,4},{6,5},{7,6},{8,7},{9,8},{10,9},{11,1... | collective-permute-start | bytes 3145736 | tf_op jit(solution)/shard_map/ppermute | solution.py:16
  352.8 107.4 %collective-permute-start.3 = (bf16[512,1024]{1,0:T(8,128)(2,1)}, bf16[512,1024]{1,0:T(8,128)(2,1)S(1)}, u32[]{:S(2)}, u32[]{:S(2)}) collective-permute-start(bf16[512,1024]{1,0:T(8,128)(2,1)} %convolution_convert_fusion.3), channel_id=1, source_target_pairs={{2,0},{3,1},{4,2},{5,3},{6,4},{7,5},{8,6},{9,7},{10,8},{11,9},{12,... | collective-permute-start | bytes 3145736 | tf_op jit(solution)/shard_map/ppermute | solution.py:16
  361.4 98.8 %copy-start.1 = (bf16[2560,1024]{1,0:T(8,128)(2,1)}, bf16[2560,1024]{1,0:T(8,128)(2,1)S(1)}, u32[]{:S(2)}) copy-start(bf16[2560,1024]{1,0:T(8,128)(2,1)S(1)} %constant_dynamic-update-slice_fusion.6) | copy-start | bytes 15728644
  361.4 101.1 %copy-start.5 = (s32[1,4]{1,0:T(1,128)S(1)}, s32[1,4]{1,0:T(1,128)}, u32[]{:S(2)}) copy-start(s32[1,4]{1,0:T(1,128)} %param.17) | copy-start | bytes 52
  460.2 2.3 copy-start.2
  477.4 1.7 copy-start
  496.7 1.7 copy-start
  516.1 1.7 copy-start
  535.4 1.7 copy-start
Sparse Core Ops, SparseCore 0:
  9.4 72.5 all-gather.5
  84.1 79.0 all-gather.3
  165.3 273.4 all-gather.7
